TPU v7x, 32 devices: a whole 2x2x4 slice. The times are simulated.
32 devices in a mesh: tm: 4 (over y, x), space: 8 (over z, core).
Axes of the slice: x: 2, y: 2, z: 4, core: 2. Of those that a mesh axis runs over, the one named last changes fastest.
Arguments:
- queries: bfloat16 [4, 768, 3072], P('tm', 'space'), may hold values from -8 to 8
- key_rows: bfloat16 [4, 768, 3072], P('tm', 'space'), may hold values from -8 to 8
- value_rows: bfloat16 [4, 768, 3072], P('tm', 'space'), may hold values from -6 to 6
- noise_level: int32 [4], P('tm'), may hold values from 0 to 999
- decay_power: int32 [24], replicated, may hold values from 0 to 7
- head_gain: float32 [24, 128], replicated, may hold values from 0.1 to 1.9
Outputs:
- attended: bfloat16 [4, 768, 3072], P('tm', 'space')
All inputs are finite; a program needn't handle non-finite values.
Results may differ from a plain program's by a relative error of at most 0.0049.
Values may be sent and summed in bfloat16 or wider, within the bound.
A program may use at most 64 MiB of HBM per device.

v0:
```python
import jax
import jax.numpy as jnp
from jax import lax
from jax.sharding import PartitionSpec as P

LEVELS = 1000
HGROUPS = 8
epsilon = 1e-06


def carried_in(value, axis, join, neutral):
    count, mine = (lax.axis_size(axis), lax.axis_index(axis))
    pieces = jax.tree.map(lambda part: lax.all_gather(part, axis), value)
    so_far = jax.tree.map(
        lambda part, zero: jnp.full_like(part, 0) + jnp.asarray(zero, part.dtype), value, neutral
    )

    def lap(position, so_far):
        longer = join(so_far, jax.tree.map(lambda part: part[position], pieces))
        return jax.tree.map(lambda new, old: jnp.where(position < mine, new, old), longer, so_far)

    return lax.fori_loop(0, count - 1, lap, so_far)


def spread_items(block, quarters, heads_total, depth):
    part_rows = block.shape[0] // quarters
    shaped = block.reshape(quarters, part_rows, heads_total, depth).transpose(0, 2, 1, 3)
    return shaped.reshape(quarters * heads_total, part_rows, depth)


def copied_items(block, quarters, heads_total, depth):
    every = block.reshape(block.shape[0], heads_total, depth).transpose(1, 0, 2)
    copied = jnp.broadcast_to(every[None], (quarters,) + every.shape)
    return copied.reshape(quarters * heads_total, block.shape[0], depth)


def attend_head(bundle):
    query, key_item, value_item, state, gain_row = bundle
    factor = query.shape[1] ** (-0.5)
    scores = jnp.dot(query, key_item.T, preferred_element_type=jnp.float32) * factor
    row_top = jnp.max(scores, axis=1, keepdims=True)
    weights = jnp.exp(scores - row_top)
    row_total = jnp.sum(weights, axis=1, keepdims=True)
    numerator = jnp.dot(
        weights.astype(jnp.bfloat16), value_item, preferred_element_type=jnp.float32
    )
    carried = jnp.dot(query, state, preferred_element_type=jnp.float32) * factor
    mixed = numerator / row_total + carried
    normed = mixed * lax.rsqrt(jnp.mean(mixed * mixed, axis=1, keepdims=True) + epsilon) * gain_row
    return normed.astype(jnp.bfloat16)


def compose(earlier, later):
    return (earlier[0] * later[0], later[0][:, None, None] * earlier[1] + later[1])


def body(queries, key_rows, value_rows, noise_level, decay_power, head_gain):
    heads_total = decay_power.shape[0]
    depth = head_gain.shape[1]
    local_rows = queries.shape[1]
    quarters = lax.axis_size("space") // HGROUPS
    grouped = heads_total // HGROUPS
    query_items = spread_items(queries[0], quarters, heads_total, depth)
    keys_sent = copied_items(key_rows[0], quarters, heads_total, depth)
    values_sent = copied_items(value_rows[0], quarters, heads_total, depth)
    query_got, keys_got, values_got = (
        lax.all_to_all(query_items, "space", split_axis=0, concat_axis=1, tiled=True),
        lax.all_to_all(keys_sent, "space", split_axis=0, concat_axis=1, tiled=True),
        lax.all_to_all(values_sent, "space", split_axis=0, concat_axis=1, tiled=True),
    )
    key_count = keys_got.shape[1]
    fresh = (
        jnp.einsum("inh,ine->ihe", keys_got, values_got, preferred_element_type=jnp.float32)
        / key_count
    )
    group_index = lax.axis_index("space") % HGROUPS
    powers = lax.dynamic_slice_in_dim(decay_power, group_index * grouped, grouped).astype(
        jnp.float32
    )
    level_now = noise_level[0].astype(jnp.float32)
    block_count = lax.axis_size("tm")
    rate = jnp.exp2(-(powers * (0.25 + 1.75 * level_now / LEVELS)) / block_count)
    zeros_state = jnp.zeros_like(fresh)
    unused_rate, before = carried_in(
        (rate, fresh), "tm", compose, (jnp.ones_like(rate), zeros_state)
    )
    state = (rate[:, None, None] * before).astype(jnp.bfloat16)
    gain_rows = lax.dynamic_slice_in_dim(head_gain, group_index * grouped, grouped)
    outcome = lax.map(attend_head, (query_got, keys_got, values_got, state, gain_rows))
    returned = lax.all_to_all(outcome, "space", split_axis=1, concat_axis=0, tiled=True)
    part_rows = local_rows // quarters
    restored = returned.reshape(quarters, heads_total, part_rows, depth).transpose(0, 2, 1, 3)
    return restored.reshape(1, local_rows, heads_total * depth)


def solution(mesh):
    in_specs = (
        P("tm", "space", None),
        P("tm", "space", None),
        P("tm", "space", None),
        P("tm"),
        P(),
        P(),
    )
    out_specs = P("tm", "space", None)
    return jax.shard_map(body, mesh=mesh, in_specs=in_specs, out_specs=out_specs, check_vma=False)
```

profile of v0, /device:TPU:0, one launch (start us, length us, event | category | flops | bytes accessed | tf_op | source)
XLA Modules:
  0.0 99.5 jit_solution(8693053812802755996)
XLA Ops:
  0.0 1.2 %copy.38 = bf16[12,8,24,128]{3,2,1,0:T(8,128)(2,1)S(1)} copy(bf16[12,8,24,128]{3,1,2,0:T(8,128)(2,1)} %bitcast.111) | data formatting | bytes 1179648
  1.2 0.9 copy.26
  2.2 6.5 %all-to-all-start.1 = ((bf16[24,96,128]{2,1,0:T(8,128)(2,1)}), bf16[24,96,128]{2,1,0:T(8,128)(2,1)S(1)}, u32[]{:S(2)}, u32[]{:S(2)}) async-start(bf16[24,96,128]{2,1,0:T(8,128)(2,1)} %copy.26), calls=%async_computation.1 | async-start | bytes 1179648 | tf_op jit(solution)/shard_map/all_to_all | solution.py:68
  8.8 0.9 copy.28
  9.7 15.7 %all-to-all-done.1 = bf16[24,96,128]{2,1,0:T(8,128)(2,1)S(1)} async-done(((bf16[24,96,128]{2,1,0:T(8,128)(2,1)}), bf16[24,96,128]{2,1,0:T(8,128)(2,1)S(1)}, u32[]{:S(2)}, u32[]{:S(2)}) %all-to-all-start.1) | async-done | bytes 589856 | tf_op jit(solution)/shard_map/all_to_all | solution.py:68
  25.4 3.5 %all-to-all-start.2 = ((bf16[24,96,128]{2,1,0:T(8,128)(2,1)}), bf16[24,96,128]{2,1,0:T(8,128)(2,1)S(1)}, u32[]{:S(2)}, u32[]{:S(2)}) async-start(bf16[24,96,128]{2,1,0:T(8,128)(2,1)} %copy.28), calls=%async_computation.2 | async-start | bytes 1179648 | tf_op jit(solution)/shard_map/all_to_all | solution.py:69
  29.6 0.6 dynamic-slice
  31.0 9.9 %all-reduce = f32[12]{0:T(128)S(1)} all-reduce(f32[12]{0:T(128)S(1)} %get-tuple-element.187), channel_id=2, replica_groups=mesh['tm'=4,'space'=8] {'tm'}, use_global_device_ids=true, to_apply=%add | all-reduce | flops 12 | bytes 96
  41.2 0.9 copy.24
  42.2 3.4 %all-to-all-done.2 = bf16[24,96,128]{2,1,0:T(8,128)(2,1)S(1)} async-done(((bf16[24,96,128]{2,1,0:T(8,128)(2,1)}), bf16[24,96,128]{2,1,0:T(8,128)(2,1)S(1)}, u32[]{:S(2)}, u32[]{:S(2)}) %all-to-all-start.2) | async-done | bytes 589856 | tf_op jit(solution)/shard_map/all_to_all | solution.py:69
  45.6 3.5 %all-to-all-start = ((bf16[24,96,128]{2,1,0:T(8,128)(2,1)}), bf16[24,96,128]{2,1,0:T(8,128)(2,1)S(1)}, u32[]{:S(2)}, u32[]{:S(2)}) async-start(bf16[24,96,128]{2,1,0:T(8,128)(2,1)} %copy.24), calls=%async_computation | async-start | bytes 1179648 | tf_op jit(solution)/shard_map/all_to_all | solution.py:67
  49.5 12.5 %all-gather.1 = f32[12,128,128]{2,1,0:T(8,128)S(1)} all-gather(f32[3,128,128]{2,1,0:T(8,128)S(1)} %convolution_multiply_fusion.1), channel_id=3, replica_groups=mesh['tm'=4,'space'=8] {'tm'}, dimensions={0}, use_global_device_ids=true | all-gather | bytes 983040 | tf_op jit(solution)/shard_map/all_gather | solution.py:13
  62.5 3.3 %all-to-all-done = bf16[24,96,128]{2,1,0:T(8,128)(2,1)S(1)} async-done(((bf16[24,96,128]{2,1,0:T(8,128)(2,1)}), bf16[24,96,128]{2,1,0:T(8,128)(2,1)S(1)}, u32[]{:S(2)}, u32[]{:S(2)}) %all-to-all-start) | async-done | bytes 589856 | tf_op jit(solution)/shard_map/all_to_all | solution.py:67
  65.9 7.7 %while.24 = (s32[]{:T(128)}, bf16[3,768,128]{1,2,0:T(8,128)(2,1)}, bf16[3,768,128]{2,1,0:T(8,128)(2,1)S(1)}, bf16[3,768,128]{2,1,0:T(8,128)(2,1)S(1)}, bf16[3,76...) while((s32[]{:T(128)}, bf16[3,768,128]{1,2,0:T(8,128)(2,1)}, ...), condition=%wide.region_6.7_spmd, body=%wide.region_2.6_spmd.sunk | while | flops 332659968 | bytes 9700445 | solution.py:89
  65.9 0.5 multiply_reduce_fusion.4
  67.1 0.6 multiply_reduce_fusion.5
  67.7 0.8 fusion.38
  69.7 0.6 multiply_reduce_fusion.5
  70.3 0.8 fusion.38
  72.2 0.6 multiply_reduce_fusion.5
  72.8 0.8 fusion.38
  73.6 1.5 %copy.31 = bf16[3,768,128]{2,0,1:T(4,128)(2,1)S(1)} copy(bf16[3,768,128]{1,2,0:T(8,128)(2,1)} %get-tuple-element.137) | data formatting | bytes 1179648 | tf_op jit(solution)/shard_map/while | solution.py:89
  75.1 23.4 %all_to_all.69 = bf16[3,768,128]{2,0,1:T(4,128)(2,1)S(1)} all-to-all(bf16[3,768,128]{2,0,1:T(4,128)(2,1)S(1)} %copy.31), channel_id=1, replica_groups=mesh['tm'=4,'space'=8] {'space'}, dimensions={1} | all-to-all | bytes 1179648 | tf_op jit(solution)/shard_map/all_to_all | solution.py:90
  98.6 1.0 copy.41
  (47 shorter events, 5.0 us)
Async XLA Ops:
  0.0 42.1 %copy-start = (f32[24,128]{1,0:T(8,128)S(1)}, f32[24,128]{1,0:T(8,128)}, u32[]{:S(2)}) copy-start(f32[24,128]{1,0:T(8,128)} %param.15) | copy-start | bytes 36868
  0.0 8.6 %copy-start.1 = (bf16[1,96,3072]{2,1,0:T(8,128)(2,1)S(1)}, bf16[1,96,3072]{2,1,0:T(8,128)(2,1)}, u32[]{:S(2)}) copy-start(bf16[1,96,3072]{2,1,0:T(8,128)(2,1)} %param.12) | copy-start | bytes 1769476
  2.1 27.4 %copy-start.4 = (u32[32]{0:T(128)S(1)}, u32[32]{0:T(128)}, u32[]{:S(2)}) copy-start(u32[32]{0:T(128)} %constant.102) | copy-start | bytes 388
  2.1 28.7 %copy-start.3 = (s32[24]{0:T(128)S(1)}, s32[24]{0:T(128)}, u32[]{:S(2)}) copy-start(s32[24]{0:T(128)} %param.14) | copy-start | bytes 292
  2.2 38.9 %copy-start.2 = (bf16[1,96,3072]{2,1,0:T(8,128)(2,1)S(1)}, bf16[1,96,3072]{2,1,0:T(8,128)(2,1)}, u32[]{:S(2)}) copy-start(bf16[1,96,3072]{2,1,0:T(8,128)(2,1)} %param.10) | copy-start | bytes 1769476
  2.2 23.2 %all-to-all-start.1 = ((bf16[24,96,128]{2,1,0:T(8,128)(2,1)}), bf16[24,96,128]{2,1,0:T(8,128)(2,1)S(1)}, u32[]{:S(2)}, u32[]{:S(2)}) async-start(bf16[24,96,128]{2,1,0:T(8,128)(2,1)} %copy.26), calls=%async_computation.1 | async-start | bytes 1179648 | tf_op jit(solution)/shard_map/all_to_all | solution.py:68
  25.4 20.2 %all-to-all-start.2 = ((bf16[24,96,128]{2,1,0:T(8,128)(2,1)}), bf16[24,96,128]{2,1,0:T(8,128)(2,1)S(1)}, u32[]{:S(2)}, u32[]{:S(2)}) async-start(bf16[24,96,128]{2,1,0:T(8,128)(2,1)} %copy.28), calls=%async_computation.2 | async-start | bytes 1179648 | tf_op jit(solution)/shard_map/all_to_all | solution.py:69
  45.6 20.2 %all-to-all-start = ((bf16[24,96,128]{2,1,0:T(8,128)(2,1)}), bf16[24,96,128]{2,1,0:T(8,128)(2,1)S(1)}, u32[]{:S(2)}, u32[]{:S(2)}) async-start(bf16[24,96,128]{2,1,0:T(8,128)(2,1)} %copy.24), calls=%async_computation | async-start | bytes 1179648 | tf_op jit(solution)/shard_map/all_to_all | solution.py:67
where the time goes:
time: 100 us; the launch traced here: 99.5 us
  blocking collectives  45.8 us (46%)
  waiting for transfers between devices  22.4 us (22%)
  starting transfers between devices  13.6 us (14%)
  local copies, waits for them, and re-layouts  7.68 us (8%)
  matrix products  4.3 us (4%)
  other arithmetic  4.18 us (4%)
  between operations  1.48 us (1%)
    all_to_all x1, blocking collectives, body(): lax.all_to_all(outcome, 'space', split_axis=1, concat_axis=0, tiled=True)  23.4 us
    all_to_all x1, waiting for transfers between devices, body(): lax.all_to_all(keys_sent, 'space', split_axis=0, concat_axis=1, tiled=True)  15.7 us
    all_gather x1, blocking collectives, carried_in(): pieces = jax.tree.map(lambda part: lax.all_gather(part, axis), value)  12.5 us
    unnamed x1, blocking collectives  9.88 us
    all_to_all x1, starting transfers between devices, body(): lax.all_to_all(keys_sent, 'space', split_axis=0, concat_axis=1, tiled=True)  6.49 us
    all_to_all x1, starting transfers between devices, body(): lax.all_to_all(values_sent, 'space', split_axis=0, concat_axis=1, tiled=T...  3.54 us
    all_to_all x1, starting transfers between devices, body(): lax.all_to_all(query_items, 'space', split_axis=0, concat_axis=1, tiled=T...  3.54 us
    all_to_all x1, waiting for transfers between devices, body(): lax.all_to_all(values_sent, 'space', split_axis=0, concat_axis=1, tiled=T...  3.4 us
  transfers between devices with their start and end apart: 3, of which 3 were waited for; matrix products, arithmetic and copies ran while one was open for 4% of the time, Pallas kernels for 0%

commit v1 on v0

--- a/solution.py
+++ b/solution.py
@@ -1,3 +1,4 @@
+import functools
 import jax
 import jax.numpy as jnp
 from jax import lax
@@ -6,6 +7,42 @@
 LEVELS = 1000
 HGROUPS = 8
 epsilon = 1e-06
+
+
+def touch_trees_now(panel, array_dim, view):
+    back = panel.shape
+    d_next = jnp.moveaxis(
+        panel.reshape(*back[:array_dim], view, back[array_dim] // view, *back[array_dim + 1 :]),
+        array_dim,
+        0,
+    )
+    return d_next
+
+
+def fix_object(vector, dim_no):
+    far_arr = list(vector.shape[1:])
+    far_arr[dim_no] *= vector.shape[0]
+    piece_out = jnp.moveaxis(vector, 0, dim_no).reshape(far_arr)
+    return piece_out
+
+
+def feed_pools(array_in, mesh_dim, t0, unit):
+    val, mid_arr = (jax.lax.axis_size(mesh_dim), jax.lax.axis_index(mesh_dim))
+    v1 = touch_trees_now(array_in, t0, val)
+    views = [v1[mid_arr]]
+    for t in tuple(range(1, val)):
+        u_next = v1[(mid_arr + t) % val]
+        views.append(
+            jax.lax.ppermute(
+                u_next, mesh_dim, [(hop_no, (hop_no + t) % val) for hop_no in range(val)]
+            )
+        )
+    v1 = jnp.stack(views)[(mid_arr - jnp.arange(val)) % val]
+    part_now = fix_object(v1, unit)
+    return part_now
+
+
+name_circles = functools.partial(feed_pools, mesh_dim="space", t0=1, unit=0)
 
 
 def carried_in(value, axis, join, neutral):
@@ -87,7 +124,7 @@
     state = (rate[:, None, None] * before).astype(jnp.bfloat16)
     gain_rows = lax.dynamic_slice_in_dim(head_gain, group_index * grouped, grouped)
     outcome = lax.map(attend_head, (query_got, keys_got, values_got, state, gain_rows))
-    returned = lax.all_to_all(outcome, "space", split_axis=1, concat_axis=0, tiled=True)
+    returned = name_circles(outcome)
     part_rows = local_rows // quarters
     restored = returned.reshape(quarters, heads_total, part_rows, depth).transpose(0, 2, 1, 3)
     return restored.reshape(1, local_rows, heads_total * depth)

time: 100 us -> 92.5 us (0.925)
  the two profiles are of different devices: /device:TPU:0 before, /device:TPU:13 now
where the time goes in v1:
time: 92.5 us; the launch traced here: 91.9 us
  starting transfers between devices  29.8 us (32%)
  waiting for transfers between devices  24.8 us (27%)
  blocking collectives  17.7 us (19%)
  local copies, waits for them, and re-layouts  11.4 us (12%)
  matrix products  4.29 us (5%)
  other arithmetic  2.15 us (2%)
  between operations  1.6 us (2%)
    all_to_all x1, waiting for transfers between devices, body(): lax.all_to_all(keys_sent, 'space', split_axis=0, concat_axis=1, tiled=True)  12.2 us
    all_gather x1, blocking collectives, carried_in(): pieces = jax.tree.map(lambda part: lax.all_gather(part, axis), value)  10.5 us
    ppermute x7, starting transfers between devices, feed_pools(): jax.lax.ppermute(u_next, mesh_dim, [(hop_no, (hop_no + t) % val) for hop_...  10.2 us
    ppermute x7, waiting for transfers between devices, feed_pools(): jax.lax.ppermute(u_next, mesh_dim, [(hop_no, (hop_no + t) % val) for hop_...  8.11 us
    unnamed x1, blocking collectives  7.16 us
    all_to_all x1, starting transfers between devices, body(): lax.all_to_all(query_items, 'space', split_axis=0, concat_axis=1, tiled=T...  6.98 us
    all_to_all x1, starting transfers between devices, body(): lax.all_to_all(values_sent, 'space', split_axis=0, concat_axis=1, tiled=T...  6.95 us
    all_to_all x1, starting transfers between devices, body(): lax.all_to_all(keys_sent, 'space', split_axis=0, concat_axis=1, tiled=True)  5.74 us
  transfers between devices with their start and end apart: 10, of which 6 were waited for; matrix products, arithmetic and copies ran while one was open for 5% of the time, Pallas kernels for 0%

profile of v1, /device:TPU:13, one launch (start us, length us, event | category | flops | bytes accessed | tf_op | source)
XLA Modules:
  0.0 91.9 jit_solution(4627879809685101602)
XLA Ops:
  0.0 1.2 %copy.35 = bf16[12,8,24,128]{3,2,1,0:T(8,128)(2,1)S(1)} copy(bf16[12,8,24,128]{3,1,2,0:T(8,128)(2,1)} %bitcast.138) | data formatting | bytes 1179648
  1.2 0.9 copy.23
  2.2 5.7 %all-to-all-start.1 = ((bf16[24,96,128]{2,1,0:T(8,128)(2,1)}), bf16[24,96,128]{2,1,0:T(8,128)(2,1)S(1)}, u32[]{:S(2)}, u32[]{:S(2)}) async-start(bf16[24,96,128]{2,1,0:T(8,128)(2,1)} %copy.23), calls=%async_computation.1 | async-start | bytes 1179648 | tf_op jit(solution)/shard_map/all_to_all | solution.py:105
  8.0 0.9 copy.25
  8.9 12.2 %all-to-all-done.1 = bf16[24,96,128]{2,1,0:T(8,128)(2,1)S(1)} async-done(((bf16[24,96,128]{2,1,0:T(8,128)(2,1)}), bf16[24,96,128]{2,1,0:T(8,128)(2,1)S(1)}, u32[]{:S(2)}, u32[]{:S(2)}) %all-to-all-start.1) | async-done | bytes 589856 | tf_op jit(solution)/shard_map/all_to_all | solution.py:105
  21.1 7.0 %all-to-all-start.2 = ((bf16[24,96,128]{2,1,0:T(8,128)(2,1)}), bf16[24,96,128]{2,1,0:T(8,128)(2,1)S(1)}, u32[]{:S(2)}, u32[]{:S(2)}) async-start(bf16[24,96,128]{2,1,0:T(8,128)(2,1)} %copy.25), calls=%async_computation.2 | async-start | bytes 1179648 | tf_op jit(solution)/shard_map/all_to_all | solution.py:106
  30.2 7.2 %all-reduce = f32[12]{0:T(128)S(1)} all-reduce(f32[12]{0:T(128)S(1)} %get-tuple-element.187), channel_id=2, replica_groups=mesh['tm'=4,'space'=8] {'tm'}, use_global_device_ids=true, to_apply=%add | all-reduce | flops 12 | bytes 96
  37.7 0.9 copy.21
  38.7 2.6 %all-to-all-done.2 = bf16[24,96,128]{2,1,0:T(8,128)(2,1)S(1)} async-done(((bf16[24,96,128]{2,1,0:T(8,128)(2,1)}), bf16[24,96,128]{2,1,0:T(8,128)(2,1)S(1)}, u32[]{:S(2)}, u32[]{:S(2)}) %all-to-all-start.2) | async-done | bytes 589856 | tf_op jit(solution)/shard_map/all_to_all | solution.py:106
  41.3 7.0 %all-to-all-start = ((bf16[24,96,128]{2,1,0:T(8,128)(2,1)}), bf16[24,96,128]{2,1,0:T(8,128)(2,1)S(1)}, u32[]{:S(2)}, u32[]{:S(2)}) async-start(bf16[24,96,128]{2,1,0:T(8,128)(2,1)} %copy.21), calls=%async_computation | async-start | bytes 1179648 | tf_op jit(solution)/shard_map/all_to_all | solution.py:104
  48.7 10.5 %all-gather.1 = f32[12,128,128]{2,1,0:T(8,128)S(1)} all-gather(f32[3,128,128]{2,1,0:T(8,128)S(1)} %convolution_multiply_fusion.1), channel_id=3, replica_groups=mesh['tm'=4,'space'=8] {'tm'}, dimensions={0}, use_global_device_ids=true | all-gather | bytes 983040 | tf_op jit(solution)/shard_map/all_gather | solution.py:50
  59.6 1.9 %all-to-all-done = bf16[24,96,128]{2,1,0:T(8,128)(2,1)S(1)} async-done(((bf16[24,96,128]{2,1,0:T(8,128)(2,1)}), bf16[24,96,128]{2,1,0:T(8,128)(2,1)S(1)}, u32[]{:S(2)}, u32[]{:S(2)}) %all-to-all-start) | async-done | bytes 589856 | tf_op jit(solution)/shard_map/all_to_all | solution.py:104
  61.6 8.2 %while.24 = (s32[]{:T(128)}, bf16[3,768,128]{2,1,0:T(8,128)(2,1)}, bf16[3,768,128]{2,1,0:T(8,128)(2,1)S(1)}, bf16[3,768,128]{2,1,0:T(8,128)(2,1)S(1)}, bf16[3,76...) while((s32[]{:T(128)}, bf16[3,768,128]{2,1,0:T(8,128)(2,1)}, ...), condition=%wide.region_6.7_spmd, body=%wide.region_2.6_spmd.sunk | while | flops 332659968 | bytes 10486877 | solution.py:126
  63.7 0.7 constant_dynamic-update-slice_fusion.2
  69.9 1.1 %dynamic-slice_bitcast_fusion.1 = (bf16[3,96,128]{2,1,0:T(8,128)(2,1)S(1)}, bf16[3,96,128]{2,1,0:T(8,128)(2,1)S(1)}, bf16[3,96,128]{2,1,0:T(8,128)(2,1)S(1)}, bf...) fusion(bf16[3,8,96,128]{3,2,1,0:T(8,128)(2,1)} %bitcast.141, ...), kind=kLoop, calls=%fused_computation.47 | loop fusion | bytes 1032220 | tf_op jit(solution)/shard_map/squeeze | solution.py:34
  71.0 1.8 %collective-permute-start = (bf16[3,96,128]{2,1,0:T(8,128)(2,1)S(1)}, bf16[3,96,128]{2,1,0:T(8,128)(2,1)S(1)}, u32[]{:S(2)}, u32[]{:S(2)}) collective-permute-start(bf16[3,96,128]{2,1,0:T(8,128)(2,1)S(1)} %get-tuple-element.199), channel_id=1, source_target_pairs={{0,1},{1,2},{2,3},{3,4},{4,5},{5,6},{6,7},{7,0},{8,9},{9,10},{10,1... | collective-permute-start | bytes 221192 | tf_op jit(solution)/shard_map/ppermute | solution.py:36
  72.8 1.9 %collective-permute-start.1 = (bf16[3,96,128]{2,1,0:T(8,128)(2,1)S(1)}, bf16[3,96,128]{2,1,0:T(8,128)(2,1)S(1)}, u32[]{:S(2)}, u32[]{:S(2)}) collective-permute-start(bf16[3,96,128]{2,1,0:T(8,128)(2,1)S(1)} %get-tuple-element.198), channel_id=1, source_target_pairs={{0,2},{1,3},{2,4},{3,5},{4,6},{5,7},{6,0},{7,1},{8,10},{9,11},{10,... | collective-permute-start | bytes 221192 | tf_op jit(solution)/shard_map/ppermute | solution.py:36
  74.7 2.4 %collective-permute-start.2 = (bf16[3,96,128]{2,1,0:T(8,128)(2,1)S(1)}, bf16[3,96,128]{2,1,0:T(8,128)(2,1)S(1)}, u32[]{:S(2)}, u32[]{:S(2)}) collective-permute-start(bf16[3,96,128]{2,1,0:T(8,128)(2,1)S(1)} %get-tuple-element.197), channel_id=1, source_target_pairs={{0,3},{1,4},{2,5},{3,6},{4,7},{5,0},{6,1},{7,2},{8,11},{9,12},{10,... | collective-permute-start | bytes 221192 | tf_op jit(solution)/shard_map/ppermute | solution.py:36
  77.0 1.7 %collective-permute-start.4 = (bf16[3,96,128]{2,1,0:T(8,128)(2,1)S(1)}, bf16[3,96,128]{2,1,0:T(8,128)(2,1)S(1)}, u32[]{:S(2)}, u32[]{:S(2)}) collective-permute-start(bf16[3,96,128]{2,1,0:T(8,128)(2,1)S(1)} %get-tuple-element.195), channel_id=1, source_target_pairs={{0,5},{1,6},{2,7},{3,0},{4,1},{5,2},{6,3},{7,4},{8,13},{9,14},{10,... | collective-permute-start | bytes 221192 | tf_op jit(solution)/shard_map/ppermute | solution.py:36
  78.7 0.9 bitcast_dynamic-update-slice_fusion.7
  79.6 2.4 %collective-permute-start.5 = (bf16[3,96,128]{2,1,0:T(8,128)(2,1)S(1)}, bf16[3,96,128]{2,1,0:T(8,128)(2,1)S(1)}, u32[]{:S(2)}, u32[]{:S(2)}) collective-permute-start(bf16[3,96,128]{2,1,0:T(8,128)(2,1)S(1)} %get-tuple-element.194), channel_id=1, source_target_pairs={{0,6},{1,7},{2,0},{3,1},{4,2},{5,3},{6,4},{7,5},{8,14},{9,15},{10,... | collective-permute-start | bytes 221192 | tf_op jit(solution)/shard_map/ppermute | solution.py:36
  82.1 3.6 %collective-permute-done.3 = bf16[3,96,128]{2,1,0:T(8,128)(2,1)S(1)} collective-permute-done((bf16[3,96,128]{2,1,0:T(8,128)(2,1)S(1)}, bf16[3,96,128]{2,1,0:T(8,128)(2,1)S(1)}, u32[]{:S(2)}, u32[]{:S(2)}) %collective-permute-start.3) | collective-permute-done | bytes 73760 | tf_op jit(solution)/shard_map/ppermute | solution.py:36
  85.7 4.5 %collective-permute-done.5 = bf16[3,96,128]{2,1,0:T(8,128)(2,1)S(1)} collective-permute-done((bf16[3,96,128]{2,1,0:T(8,128)(2,1)S(1)}, bf16[3,96,128]{2,1,0:T(8,128)(2,1)S(1)}, u32[]{:S(2)}, u32[]{:S(2)}) %collective-permute-start.5) | collective-permute-done | bytes 73760 | tf_op jit(solution)/shard_map/ppermute | solution.py:36
  91.0 1.0 %copy.38 = bf16[1,24,12,8,128]{4,3,1,2,0:T(8,128)(2,1)} copy(bf16[1,24,12,8,128]{4,3,2,1,0:T(8,128)(2,1)S(1)} %bitcast.132) | data formatting | bytes 1179648 | tf_op jit(solution)/shard_map/reshape | solution.py:130
  (75 shorter events, 10.8 us)
Async XLA Ops:
  0.0 38.6 %copy-start = (f32[24,128]{1,0:T(8,128)S(1)}, f32[24,128]{1,0:T(8,128)}, u32[]{:S(2)}) copy-start(f32[24,128]{1,0:T(8,128)} %param.15) | copy-start | bytes 36868
  0.0 7.9 %copy-start.1 = (bf16[1,96,3072]{2,1,0:T(8,128)(2,1)S(1)}, bf16[1,96,3072]{2,1,0:T(8,128)(2,1)}, u32[]{:S(2)}) copy-start(bf16[1,96,3072]{2,1,0:T(8,128)(2,1)} %param.12) | copy-start | bytes 1769476
  2.1 26.6 %copy-start.4 = (u32[32]{0:T(128)S(1)}, u32[32]{0:T(128)}, u32[]{:S(2)}) copy-start(u32[32]{0:T(128)} %constant.151) | copy-start | bytes 388
  2.1 27.9 %copy-start.3 = (s32[24]{0:T(128)S(1)}, s32[24]{0:T(128)}, u32[]{:S(2)}) copy-start(s32[24]{0:T(128)} %param.14) | copy-start | bytes 292
  2.2 35.4 %copy-start.2 = (bf16[1,96,3072]{2,1,0:T(8,128)(2,1)S(1)}, bf16[1,96,3072]{2,1,0:T(8,128)(2,1)}, u32[]{:S(2)}) copy-start(bf16[1,96,3072]{2,1,0:T(8,128)(2,1)} %param.10) | copy-start | bytes 1769476
  2.2 19.0 %all-to-all-start.1 = ((bf16[24,96,128]{2,1,0:T(8,128)(2,1)}), bf16[24,96,128]{2,1,0:T(8,128)(2,1)S(1)}, u32[]{:S(2)}, u32[]{:S(2)}) async-start(bf16[24,96,128]{2,1,0:T(8,128)(2,1)} %copy.23), calls=%async_computation.1 | async-start | bytes 1179648 | tf_op jit(solution)/shard_map/all_to_all | solution.py:105
  21.1 20.2 %all-to-all-start.2 = ((bf16[24,96,128]{2,1,0:T(8,128)(2,1)}), bf16[24,96,128]{2,1,0:T(8,128)(2,1)S(1)}, u32[]{:S(2)}, u32[]{:S(2)}) async-start(bf16[24,96,128]{2,1,0:T(8,128)(2,1)} %copy.25), calls=%async_computation.2 | async-start | bytes 1179648 | tf_op jit(solution)/shard_map/all_to_all | solution.py:106
  41.3 20.2 %all-to-all-start = ((bf16[24,96,128]{2,1,0:T(8,128)(2,1)}), bf16[24,96,128]{2,1,0:T(8,128)(2,1)S(1)}, u32[]{:S(2)}, u32[]{:S(2)}) async-start(bf16[24,96,128]{2,1,0:T(8,128)(2,1)} %copy.21), calls=%async_computation | async-start | bytes 1179648 | tf_op jit(solution)/shard_map/all_to_all | solution.py:104
  71.0 8.6 %collective-permute-start = (bf16[3,96,128]{2,1,0:T(8,128)(2,1)S(1)}, bf16[3,96,128]{2,1,0:T(8,128)(2,1)S(1)}, u32[]{:S(2)}, u32[]{:S(2)}) collective-permute-start(bf16[3,96,128]{2,1,0:T(8,128)(2,1)S(1)} %get-tuple-element.199), channel_id=1, source_target_pairs={{0,1},{1,2},{2,3},{3,4},{4,5},{5,6},{6,7},{7,0},{8,9},{9,10},{10,1... | collective-permute-start | bytes 221192 | tf_op jit(solution)/shard_map/ppermute | solution.py:36
  72.8 9.3 %collective-permute-start.1 = (bf16[3,96,128]{2,1,0:T(8,128)(2,1)S(1)}, bf16[3,96,128]{2,1,0:T(8,128)(2,1)S(1)}, u32[]{:S(2)}, u32[]{:S(2)}) collective-permute-start(bf16[3,96,128]{2,1,0:T(8,128)(2,1)S(1)} %get-tuple-element.198), channel_id=1, source_target_pairs={{0,2},{1,3},{2,4},{3,5},{4,6},{5,7},{6,0},{7,1},{8,10},{9,11},{10,... | collective-permute-start | bytes 221192 | tf_op jit(solution)/shard_map/ppermute | solution.py:36
  74.7 7.5 %collective-permute-start.2 = (bf16[3,96,128]{2,1,0:T(8,128)(2,1)S(1)}, bf16[3,96,128]{2,1,0:T(8,128)(2,1)S(1)}, u32[]{:S(2)}, u32[]{:S(2)}) collective-permute-start(bf16[3,96,128]{2,1,0:T(8,128)(2,1)S(1)} %get-tuple-element.197), channel_id=1, source_target_pairs={{0,3},{1,4},{2,5},{3,6},{4,7},{5,0},{6,1},{7,2},{8,11},{9,12},{10,... | collective-permute-start | bytes 221192 | tf_op jit(solution)/shard_map/ppermute | solution.py:36
  77.0 8.7 %collective-permute-start.3 = (bf16[3,96,128]{2,1,0:T(8,128)(2,1)S(1)}, bf16[3,96,128]{2,1,0:T(8,128)(2,1)S(1)}, u32[]{:S(2)}, u32[]{:S(2)}) collective-permute-start(bf16[3,96,128]{2,1,0:T(8,128)(2,1)S(1)} %get-tuple-element.196), channel_id=1, source_target_pairs={{0,4},{1,5},{2,6},{3,7},{4,0},{5,1},{6,2},{7,3},{8,12},{9,13},{10,... | collective-permute-start | bytes 221192 | tf_op jit(solution)/shard_map/ppermute | solution.py:36
  77.0 8.7 %collective-permute-start.4 = (bf16[3,96,128]{2,1,0:T(8,128)(2,1)S(1)}, bf16[3,96,128]{2,1,0:T(8,128)(2,1)S(1)}, u32[]{:S(2)}, u32[]{:S(2)}) collective-permute-start(bf16[3,96,128]{2,1,0:T(8,128)(2,1)S(1)} %get-tuple-element.195), channel_id=1, source_target_pairs={{0,5},{1,6},{2,7},{3,0},{4,1},{5,2},{6,3},{7,4},{8,13},{9,14},{10,... | collective-permute-start | bytes 221192 | tf_op jit(solution)/shard_map/ppermute | solution.py:36
  79.6 10.6 %collective-permute-start.5 = (bf16[3,96,128]{2,1,0:T(8,128)(2,1)S(1)}, bf16[3,96,128]{2,1,0:T(8,128)(2,1)S(1)}, u32[]{:S(2)}, u32[]{:S(2)}) collective-permute-start(bf16[3,96,128]{2,1,0:T(8,128)(2,1)S(1)} %get-tuple-element.194), channel_id=1, source_target_pairs={{0,6},{1,7},{2,0},{3,1},{4,2},{5,3},{6,4},{7,5},{8,14},{9,15},{10,... | collective-permute-start | bytes 221192 | tf_op jit(solution)/shard_map/ppermute | solution.py:36
  82.0 8.3 %collective-permute-start.6 = (bf16[3,96,128]{2,1,0:T(8,128)(2,1)S(1)}, bf16[3,96,128]{2,1,0:T(8,128)(2,1)S(1)}, u32[]{:S(2)}, u32[]{:S(2)}) collective-permute-start(bf16[3,96,128]{2,1,0:T(8,128)(2,1)S(1)} %get-tuple-element.193), channel_id=1, source_target_pairs={{0,7},{1,0},{2,1},{3,2},{4,3},{5,4},{6,5},{7,6},{8,15},{9,8},{10,9... | collective-permute-start | bytes 221192 | tf_op jit(solution)/shard_map/ppermute | solution.py:36
